TPU v7x, 256 devices: a whole 4x4x8 slice. The times are simulated.
256 devices in a mesh: grp: 8 (over y, core), sub: 32 (over x, z).
Axes of the slice: x: 4, y: 4, z: 8, core: 2. Of those that a mesh axis runs over, the one named last changes fastest.
Arguments:
- right_side: float32 [65536, 2048], P(('grp', 'sub'))
- schur: bfloat16 [131072, 512], P(('grp', 'sub'))
- inv_factor: bfloat16 [131072, 512], P(('grp', 'sub'))
- coarse_inverse: float32 [2048, 256], P('grp')
- primal_index: int32 [256, 8], P(('grp', 'sub')), may hold values from 0 to 255
- phase: int32 [65536], P(('grp', 'sub')), may hold values from 0 to 3
- phase_coef: float32 [4], replicated, may hold values from 0.5 to 4
Outputs:
- solution: float32 [65536, 2048], P(('grp', 'sub'))
- residual: float32 [65536, 2048], P(('grp', 'sub'))
All inputs are finite; a program needn't handle non-finite values.
Results may differ from a plain program's by a relative error of at most 0.0056.
Values may be sent and summed in bfloat16 or wider, within the bound.
A program may use at most 64 MiB of HBM per device.

v0:
```python
import jax
import jax.numpy as jnp
from jax import lax
from jax.sharding import PartitionSpec as P


def shifted(value, axis, steps):
    count = lax.axis_size(axis)
    pairs = [(source, (source + steps) % count) for source in range(count)]
    return lax.ppermute(value, axis, pairs)


def transposed(matrix, operand):
    return lax.dot_general(
        matrix, operand, (((0,), (0,)), ((), ())), preferred_element_type=jnp.float32
    )


def body(right_side, schur, inv_factor, coarse_inverse, primal_index, phase, phase_coef):
    highest = lax.Precision.HIGHEST
    face_rows = right_side.shape[0]
    columns = jnp.arange(face_rows, dtype=jnp.int32)
    onehot = (primal_index[0][:, None] == columns[None, :]).astype(jnp.float32)
    primal_count = onehot.shape[0]
    resid_b = right_side.astype(jnp.bfloat16)
    left_resid = shifted(resid_b, "sub", 1)
    local_resid = jnp.concatenate([left_resid, resid_b], axis=0)
    first = jnp.dot(inv_factor, local_resid, preferred_element_type=jnp.float32).astype(
        jnp.bfloat16
    )
    second = transposed(inv_factor, first).astype(jnp.bfloat16)
    upper = second[:face_rows]
    from_right = shifted(upper, "sub", -1)
    lower = second[face_rows:]
    local_part = lower.astype(jnp.float32) + from_right.astype(jnp.float32)
    own_primal = jnp.dot(onehot, right_side, precision=highest)
    position = lax.axis_index("sub")
    group_primal = lax.all_gather(own_primal, "sub", axis=0, tiled=True)
    my_rows = lax.dynamic_slice_in_dim(coarse_inverse, position * primal_count, primal_count, 0)
    solved = jnp.dot(my_rows, group_primal, precision=highest)
    summed = lax.psum(solved, "grp")
    correction = solved + summed / lax.axis_size("grp")
    scattered = lax.dot_general(onehot, correction, (((0,), (0,)), ((), ())), precision=highest)
    direction = 0.5 * local_part + scattered
    dir_b = direction.astype(jnp.bfloat16)
    rz_part = jnp.sum(right_side * direction, axis=0)
    left_dir = shifted(dir_b, "sub", 1)
    image = jnp.dot(
        schur, jnp.concatenate([left_dir, dir_b], axis=0), preferred_element_type=jnp.float32
    ).astype(jnp.bfloat16)
    image_up = image[:face_rows]
    image_right = shifted(image_up, "sub", -1)
    image_low = image[face_rows:]
    phase_table = (
        phase[:, None] == jnp.arange(phase_coef.shape[0], dtype=jnp.int32)[None, :]
    ).astype(jnp.float32)
    coef_rows = jnp.dot(phase_table, phase_coef, precision=highest)
    dir_f = dir_b.astype(jnp.float32)
    qvec = (
        image_low.astype(jnp.float32) + image_right.astype(jnp.float32) + coef_rows[:, None] * dir_f
    )
    pq_part = jnp.sum(dir_f * qvec, axis=0)
    rz_total, pq_total = lax.psum((rz_part, pq_part), ("grp", "sub"))
    alpha = rz_total / pq_total
    return (alpha * dir_f, right_side - alpha * qvec)


def solution(mesh):
    in_specs = (
        P(("grp", "sub"), None),
        P(("grp", "sub"), None),
        P(("grp", "sub"), None),
        P("grp", None),
        P(("grp", "sub"), None),
        P(("grp", "sub")),
        P(),
    )
    out_specs = (P(("grp", "sub"), None), P(("grp", "sub"), None))
    return jax.shard_map(body, mesh=mesh, in_specs=in_specs, out_specs=out_specs, check_vma=False)
```

profile of v0, /device:TPU:1, one launch (start us, length us, event | category | flops | bytes accessed | tf_op | source)
XLA Modules:
  0.0 310.6 jit_solution(18175832615231809562)
XLA Ops:
  7.2 0.0 copy-start
  7.2 0.0 copy-start.1
  7.2 0.0 all-gather.2.cloned.1.call-start
  7.2 3.2 %fusion.21 = f32[8,2048]{1,0:T(8,128)} fusion(f32[256,2048]{1,0:T(8,128)} %param.7, s32[8]{0:T(128)} %bitcast.16), kind=kOutput, calls=%fused_computation.30 | convolution fusion | flops 50333696 | bytes 2162720 | tf_op jit(solution)/shard_map/dot_general | solution.py:36
  10.4 0.0 all-gather.2.cloned.1.call-update
  10.4 0.0 all-reduce.3.cloned.1.call-start
  10.5 0.0 copy-done.1
  10.5 0.1 convert_element_type.39
  10.6 0.0 copy-start.6
  10.6 1.0 copy-done.6
  11.6 2.5 collective-permute-start
  14.1 30.4 %collective-permute-done = bf16[256,2048]{1,0:T(8,128)(2,1)} collective-permute-done((bf16[256,2048]{1,0:T(8,128)(2,1)S(1)}, bf16[256,2048]{1,0:T(8,128)(2,1)}, u32[]{:S(2)}, u32[]{:S(2)}) %collective-permute-start) | collective-permute-done | bytes 1048608 | tf_op jit(solution)/shard_map/ppermute | solution.py:10
  44.5 0.0 copy-done
  44.5 5.3 %fusion = bf16[512,2048]{1,0:T(8,128)(2,1)} fusion(bf16[512,512]{1,0:T(8,128)(2,1)S(1)} %copy-done, bf16[256,2048]{1,0:T(8,128)(2,1)} %copy-done.6, bf16[256,2048]{1,0:T(8,128)(2,1)} %collective-permute-done), kind=kOutput, calls=%fused_computation.6 | convolution fusion | flops 2153775104 | bytes 4718592 | tf_op jit(solution)/shard_map/dot_general | solution.py:14
  49.8 0.0 copy-start.7
  49.8 2.3 slice.17
  52.1 1.3 collective-permute-start.1
  53.4 39.7 %all-gather.2.cloned.1.call-done = f32[256,2048]{1,0:T(8,128)} async-done(((f32[8,2048]{1,0:T(8,128)}), f32[256,2048]{1,0:T(8,128)}) %all-gather.2.cloned.1.call-update) | async-done | bytes 2097168 | tf_op jit(solution)/shard_map/all_gather | solution.py:38
  93.1 3.3 %fusion.19 = f32[8,2048]{1,0:T(8,128)} fusion(f32[256,2048]{1,0:T(8,128)} %all-gather.2.cloned.1.call-done, f32[256,256]{1,0:T(8,128)} %param.10, s32[]{:T(128)S(6)} %select_n.3), kind=kOutput, calls=%fused_computation.27 | convolution fusion | flops 50331648 | bytes 2170884 | tf_op jit(solution)/shard_map/dot_general | solution.py:40
  96.4 0.0 all-reduce.3.cloned.1.call-update
  96.4 65.5 %all-reduce.3.cloned.1.call-done = f32[8,2048]{1,0:T(8,128)} async-done(((f32[8,2048]{1,0:T(8,128)}), f32[8,2048]{1,0:T(8,128)}) %all-reduce.3.cloned.1.call-update) | async-done | bytes 65552 | tf_op jit(solution)/shard_map/psum | solution.py:41
  161.9 0.0 copy-done.7
  161.9 0.0 copy-start.5
  162.0 2.1 fusion.15
  164.1 0.0 copy-start.8
  164.1 0.0 collective-permute-done.1
  164.1 0.0 copy-done.5
  164.1 1.9 multiply_reduce_fusion
  166.0 0.0 copy-start.2
  166.0 1.2 collective-permute-start.2
  167.2 24.4 %collective-permute-done.2 = bf16[256,2048]{1,0:T(8,128)(2,1)S(1)} collective-permute-done((bf16[256,2048]{1,0:T(8,128)(2,1)S(1)}, bf16[256,2048]{1,0:T(8,128)(2,1)S(1)}, u32[]{:S(2)}, u32[]{:S(2)}) %collective-permute-start.2) | collective-permute-done | bytes 1048608 | tf_op jit(solution)/shard_map/ppermute | solution.py:10
  191.7 0.0 copy-done.8
  191.7 1.3 fusion.1
  192.9 0.0 copy-start.3
  193.0 0.0 copy-start.9
  193.0 0.0 copy-start.10
  193.0 0.1 slice.19
  193.1 1.3 collective-permute-start.3
  194.3 0.0 copy-done.9
  194.3 0.0 copy-done.10
  194.4 0.2 fusion.13
  194.5 19.8 %collective-permute-done.3 = bf16[256,2048]{1,0:T(8,128)(2,1)S(1)} collective-permute-done((bf16[256,2048]{1,0:T(8,128)(2,1)S(1)}, bf16[256,2048]{1,0:T(8,128)(2,1)S(1)}, u32[]{:S(2)}, u32[]{:S(2)}) %collective-permute-start.3) | collective-permute-done | bytes 1048608 | tf_op jit(solution)/shard_map/ppermute | solution.py:10
  214.3 0.0 copy-done.2
  214.3 0.7 fusion.3
  215.0 0.0 copy-done.3
  215.0 0.3 copy-done.4
  215.3 83.7 %all-reduce = (f32[2048]{0:T(1024)S(1)}, f32[2048]{0:T(1024)S(1)}) all-reduce(f32[2048]{0:T(1024)S(1)} %get-tuple-element.4, f32[2048]{0:T(1024)S(1)} %fusion.3), channel_id=1, replica_groups=mesh['grp'=8,'sub'=32] {'grp','sub'}, use_global_device_ids=true, to_apply=%region_2.0 | all-reduce | flops 4096 | bytes 32768 | tf_op jit(solution)/shard_map/psum | solution.py:63
  299.0 4.8 %multiply_subtract_fusion = (f32[256,2048]{1,0:T(8,128)}, f32[256,2048]{1,0:T(8,128)}) fusion(f32[256,2048]{1,0:T(8,128)S(1)} %copy-done.1, bf16[256,2048]{1,0:T(8,128)(2,1)} %copy-done.2, bf16[256,2048]{1,0:T(8,128)(2,1)} %copy-done.4, f32[2048]{0:T(1024)S(1)} %div.11, f32[256]{0:T(256)S(1)} %bitcast.15, bf16[512,2048]{1,0:T(8,128)(2,1)} %copy-done.3), kind=kLoop, calls=%fused_computation.16 | loop fusion | flops 4718592 | bytes 9446400 | tf_op jit(solution)/shard_map/sub | solution.py:65
  (2 shorter events, 0.0 us)
Async XLA Ops:
  7.2 37.3 %copy-start = (bf16[512,512]{1,0:T(8,128)(2,1)S(1)}, bf16[512,512]{1,0:T(8,128)(2,1)}, u32[]{:S(2)}) copy-start(bf16[512,512]{1,0:T(8,128)(2,1)} %param.9) | copy-start | bytes 1572868
  7.2 3.3 %copy-start.1 = (f32[256,2048]{1,0:T(8,128)S(1)}, f32[256,2048]{1,0:T(8,128)}, u32[]{:S(2)}) copy-start(f32[256,2048]{1,0:T(8,128)} %param.7) | copy-start | bytes 6291460
  7.2 85.9 %all-gather.2.cloned.1.call-start = ((), (), s32[]{:S(2)}) async-start(), calls=%async_computation | async-start | bytes 2162688 | tf_op jit(solution)/shard_map/all_gather | solution.py:38
  10.4 151.5 %all-reduce.3.cloned.1.call-start = ((), (), s32[]{:S(2)}) async-start(), calls=%async_computation.1 | async-start | bytes 131072 | tf_op jit(solution)/shard_map/psum | solution.py:41
  10.6 1.0 copy-start.6
  11.6 32.9 %collective-permute-start = (bf16[256,2048]{1,0:T(8,128)(2,1)S(1)}, bf16[256,2048]{1,0:T(8,128)(2,1)}, u32[]{:S(2)}, u32[]{:S(2)}) collective-permute-start(bf16[256,2048]{1,0:T(8,128)(2,1)S(1)} %convert_element_type.39), channel_id=1, source_target_pairs={{0,1},{1,2},{2,3},{3,4},{4,5},{5,6},{6,7},{7,8},{8,9},{9,10},{10,1... | collective-permute-start | bytes 3145736 | tf_op jit(solution)/shard_map/ppermute | solution.py:10
  49.8 112.2 %copy-start.7 = (s32[1,8]{1,0:T(1,128)S(1)}, s32[1,8]{1,0:T(1,128)}, u32[]{:S(2)}) copy-start(s32[1,8]{1,0:T(1,128)} %param.11) | copy-start | bytes 100
  52.1 112.0 %collective-permute-start.1 = (bf16[256,2048]{1,0:T(8,128)(2,1)}, bf16[256,2048]{1,0:T(8,128)(2,1)}, u32[]{:S(2)}, u32[]{:S(2)}) collective-permute-start(bf16[256,2048]{1,0:T(8,128)(2,1)} %slice.17), channel_id=1, source_target_pairs={{0,31},{1,0},{2,1},{3,2},{4,3},{5,4},{6,5},{7,6},{8,7},{9,8},{10,9... | collective-permute-start | bytes 3145736 | tf_op jit(solution)/shard_map/ppermute | solution.py:10
  161.9 2.1 copy-start.5
  164.1 27.6 %copy-start.8 = (bf16[512,512]{1,0:T(8,128)(2,1)S(1)}, bf16[512,512]{1,0:T(8,128)(2,1)}, u32[]{:S(2)}) copy-start(bf16[512,512]{1,0:T(8,128)(2,1)} %param.8) | copy-start | bytes 1572868
  166.0 48.3 %copy-start.2 = (bf16[256,2048]{1,0:T(8,128)(2,1)}, bf16[256,2048]{1,0:T(8,128)(2,1)S(1)}, u32[]{:S(2)}) copy-start(bf16[256,2048]{1,0:T(8,128)(2,1)S(1)} %get-tuple-element.5) | copy-start | bytes 3145732
  166.0 25.7 %collective-permute-start.2 = (bf16[256,2048]{1,0:T(8,128)(2,1)S(1)}, bf16[256,2048]{1,0:T(8,128)(2,1)S(1)}, u32[]{:S(2)}, u32[]{:S(2)}) collective-permute-start(bf16[256,2048]{1,0:T(8,128)(2,1)S(1)} %get-tuple-element.5), channel_id=1, source_target_pairs={{0,1},{1,2},{2,3},{3,4},{4,5},{5,6},{6,7},{7,8},{8,9},{9,10},{10,1... | collective-permute-start | bytes 3145736 | tf_op jit(solution)/shard_map/ppermute | solution.py:10
  192.9 22.1 %copy-start.3 = (bf16[512,2048]{1,0:T(8,128)(2,1)}, bf16[512,2048]{1,0:T(8,128)(2,1)S(1)}, u32[]{:S(2)}) copy-start(bf16[512,2048]{1,0:T(8,128)(2,1)S(1)} %fusion.1) | copy-start | bytes 6291460
  193.0 1.4 copy-start.9
  193.0 1.4 copy-start.10
  193.1 21.2 %collective-permute-start.3 = (bf16[256,2048]{1,0:T(8,128)(2,1)S(1)}, bf16[256,2048]{1,0:T(8,128)(2,1)S(1)}, u32[]{:S(2)}, u32[]{:S(2)}) collective-permute-start(bf16[256,2048]{1,0:T(8,128)(2,1)S(1)} %slice.19), channel_id=1, source_target_pairs={{0,31},{1,0},{2,1},{3,2},{4,3},{5,4},{6,5},{7,6},{8,7},{9,8},{10,9... | collective-permute-start | bytes 3145736 | tf_op jit(solution)/shard_map/ppermute | solution.py:10
  214.3 1.0 copy-start.4
Sparse Core Ops, SparseCore 0:
  10.6 82.4 all-gather.1
  96.6 65.3 all-reduce.2
where the time goes:
time: 311 us
  waiting for transfers between devices  180 us (58%)
  blocking collectives  83.7 us (27%)
  matrix products  15.3 us (5%)
  between operations  14.2 us (5%)
  other arithmetic  7.52 us (2%)
  starting transfers between devices  6.3 us (2%)
  local copies, waits for them, and re-layouts  3.72 us (1%)
    psum x1, blocking collectives, body(): rz_total, pq_total = lax.psum((rz_part, pq_part), ('grp', 'sub'))  83.7 us
    ppermute x4, waiting for transfers between devices, shifted(): return lax.ppermute(value, axis, pairs)  74.7 us
    psum x1, waiting for transfers between devices, body(): summed = lax.psum(solved, 'grp')  65.5 us
    all_gather x1, waiting for transfers between devices, body(): group_primal = lax.all_gather(own_primal, 'sub', axis=0, tiled=True)  39.7 us
  transfers between devices with their start and end apart: 6, of which 5 were waited for; matrix products, arithmetic and copies ran while one was open for 4% of the time, Pallas kernels for 0%

commit v1 on v0

--- a/solution.py
+++ b/solution.py
@@ -38,7 +38,7 @@
     group_primal = lax.all_gather(own_primal, "sub", axis=0, tiled=True)
     my_rows = lax.dynamic_slice_in_dim(coarse_inverse, position * primal_count, primal_count, 0)
     solved = jnp.dot(my_rows, group_primal, precision=highest)
-    summed = lax.psum(solved, "grp")
+    summed = jnp.sum(lax.all_gather(solved, "grp"), axis=0)
     correction = solved + summed / lax.axis_size("grp")
     scattered = lax.dot_general(onehot, correction, (((0,), (0,)), ((), ())), precision=highest)
     direction = 0.5 * local_part + scattered

time: 311 us -> 260 us (0.84)
  waiting for transfers between devices: 180 us -> 120 us
  blocking collectives: 83.7 us -> 93.1 us
    psum x1 -> x0, waiting for transfers between devices: 65.5 us -> none  [body(): summed = lax.psum(solved, 'grp')]
    all_gather x0 -> x1, blocking collectives: none -> 16.6 us  [body(): summed = jnp.sum(lax.all_gather(solved, 'grp'), axis=0)]
    psum x1, blocking collectives: 83.7 us -> 76.4 us  [body(): rz_total, pq_total = lax.psum((rz_part, pq_part), ('grp', 'sub'))]
    ppermute x4, waiting for transfers between devices: 74.7 us -> 80.5 us  [shifted(): return lax.ppermute(value, axis, pairs)]
  transfers between devices with their start and end apart: 6 -> 5, of which waited for: 5 -> 4; matrix products, arithmetic and copies ran while one was open for 4% -> 5% of each run, Pallas kernels for 0% -> 0%
where the time goes in v1:
time: 260 us; the launch traced here: 259 us
  waiting for transfers between devices  120 us (46%)
  blocking collectives  93.1 us (36%)
  between operations  14.2 us (5%)
  matrix products  13.7 us (5%)
  other arithmetic  7.55 us (3%)
  starting transfers between devices  6.83 us (3%)
  local copies, waits for them, and re-layouts  3.7 us (1%)
    ppermute x4, waiting for transfers between devices, shifted(): return lax.ppermute(value, axis, pairs)  80.5 us
    psum x1, blocking collectives, body(): rz_total, pq_total = lax.psum((rz_part, pq_part), ('grp', 'sub'))  76.4 us
    all_gather x1, waiting for transfers between devices, body(): group_primal = lax.all_gather(own_primal, 'sub', axis=0, tiled=True)  39.7 us
    all_gather x1, blocking collectives, body(): summed = jnp.sum(lax.all_gather(solved, 'grp'), axis=0)  16.6 us
    ppermute x4, starting transfers between devices, shifted(): return lax.ppermute(value, axis, pairs)  6.79 us
    dot_general x1, matrix products, transposed(): lax.dot_general(matrix, operand, (((0,), (0,)), ((), ())), preferred_elem...  5.26 us
  transfers between devices with their start and end apart: 5, of which 4 were waited for; matrix products, arithmetic and copies ran while one was open for 5% of the time, Pallas kernels for 0%

profile of v1, /device:TPU:1, one launch (start us, length us, event | category | flops | bytes accessed | tf_op | source)
XLA Modules:
  0.0 259.2 jit_solution(15024850295529538025)
XLA Ops:
  7.2 0.0 copy-start
  7.2 0.0 copy-start.1
  7.2 0.0 all-gather.3.cloned.1.call-start
  7.2 3.1 %fusion.21 = f32[8,2048]{1,0:T(8,128)} fusion(f32[256,2048]{1,0:T(8,128)} %param.7, s32[8]{0:T(128)} %bitcast.18), kind=kOutput, calls=%fused_computation.31 | convolution fusion | flops 50333696 | bytes 2162720 | tf_op jit(solution)/shard_map/dot_general | solution.py:36
  10.4 0.0 all-gather.3.cloned.1.call-update
  10.4 0.0 copy-done.1
  10.4 0.1 convert_element_type.39
  10.6 0.0 copy-start.6
  10.6 1.0 copy-done.6
  11.5 2.5 collective-permute-start
  14.0 30.4 %collective-permute-done = bf16[256,2048]{1,0:T(8,128)(2,1)} collective-permute-done((bf16[256,2048]{1,0:T(8,128)(2,1)S(1)}, bf16[256,2048]{1,0:T(8,128)(2,1)}, u32[]{:S(2)}, u32[]{:S(2)}) %collective-permute-start) | collective-permute-done | bytes 1048608 | tf_op jit(solution)/shard_map/ppermute | solution.py:10
  44.4 0.0 copy-done
  44.4 5.3 %fusion = bf16[512,2048]{1,0:T(8,128)(2,1)} fusion(bf16[512,512]{1,0:T(8,128)(2,1)S(1)} %copy-done, bf16[256,2048]{1,0:T(8,128)(2,1)} %copy-done.6, bf16[256,2048]{1,0:T(8,128)(2,1)} %collective-permute-done), kind=kOutput, calls=%fused_computation.6 | convolution fusion | flops 2153775104 | bytes 4718592 | tf_op jit(solution)/shard_map/dot_general | solution.py:14
  49.7 2.3 slice.17
  52.0 0.0 copy-start.7
  52.0 1.3 collective-permute-start.1
  53.3 39.7 %all-gather.3.cloned.1.call-done = f32[256,2048]{1,0:T(8,128)} async-done(((f32[8,2048]{1,0:T(8,128)}), f32[256,2048]{1,0:T(8,128)}) %all-gather.3.cloned.1.call-update) | async-done | bytes 2097168 | tf_op jit(solution)/shard_map/all_gather | solution.py:38
  93.0 2.7 %fusion.19 = f32[8,2048]{1,0:T(8,128)S(1)} fusion(f32[256,2048]{1,0:T(8,128)} %all-gather.3.cloned.1.call-done, f32[256,256]{1,0:T(8,128)} %param.10, s32[]{:T(128)S(6)} %select_n.3), kind=kOutput, calls=%fused_computation.28 | convolution fusion | flops 50331648 | bytes 2170884 | tf_op jit(solution)/shard_map/dot_general | solution.py:40
  95.7 0.0 copy-start.5
  95.7 16.6 %all-gather = f32[64,2048]{1,0:T(8,128)S(1)} all-gather(f32[8,2048]{1,0:T(8,128)S(1)} %fusion.19), channel_id=2, replica_groups=mesh['grp'=8,'sub'=32] {'grp'}, dimensions={0}, use_global_device_ids=true | all-gather | bytes 589824 | tf_op jit(solution)/shard_map/all_gather | solution.py:41
  112.4 0.0 copy-done.7
  112.4 1.1 fusion.15
  113.5 0.0 copy-start.8
  113.5 0.0 collective-permute-done.1
  113.5 0.0 copy-done.5
  113.5 1.9 multiply_reduce_fusion
  115.4 0.0 copy-start.2
  115.4 1.8 collective-permute-start.2
  117.2 27.5 %collective-permute-done.2 = bf16[256,2048]{1,0:T(8,128)(2,1)S(1)} collective-permute-done((bf16[256,2048]{1,0:T(8,128)(2,1)S(1)}, bf16[256,2048]{1,0:T(8,128)(2,1)S(1)}, u32[]{:S(2)}, u32[]{:S(2)}) %collective-permute-start.2) | collective-permute-done | bytes 1048608 | tf_op jit(solution)/shard_map/ppermute | solution.py:10
  144.7 0.0 copy-done.8
  144.7 1.3 fusion.1
  146.0 0.0 copy-start.3
  146.0 0.0 copy-start.9
  146.0 0.0 copy-start.10
  146.0 0.1 slice.19
  146.1 1.3 collective-permute-start.3
  147.4 0.0 copy-done.9
  147.4 0.0 copy-done.10
  147.4 0.2 fusion.13
  147.6 22.6 %collective-permute-done.3 = bf16[256,2048]{1,0:T(8,128)(2,1)S(1)} collective-permute-done((bf16[256,2048]{1,0:T(8,128)(2,1)S(1)}, bf16[256,2048]{1,0:T(8,128)(2,1)S(1)}, u32[]{:S(2)}, u32[]{:S(2)}) %collective-permute-start.3) | collective-permute-done | bytes 1048608 | tf_op jit(solution)/shard_map/ppermute | solution.py:10
  170.2 0.0 copy-start.4
  170.2 0.0 copy-done.2
  170.2 0.7 fusion.3
  170.9 0.0 copy-done.3
  170.9 0.3 copy-done.4
  171.2 76.4 %all-reduce = (f32[2048]{0:T(1024)S(1)}, f32[2048]{0:T(1024)S(1)}) all-reduce(f32[2048]{0:T(1024)S(1)} %get-tuple-element.4, f32[2048]{0:T(1024)S(1)} %fusion.3), channel_id=1, replica_groups=mesh['grp'=8,'sub'=32] {'grp','sub'}, use_global_device_ids=true, to_apply=%region_2.0 | all-reduce | flops 4096 | bytes 32768 | tf_op jit(solution)/shard_map/psum | solution.py:63
  247.6 4.8 %multiply_subtract_fusion = (f32[256,2048]{1,0:T(8,128)}, f32[256,2048]{1,0:T(8,128)}) fusion(f32[256,2048]{1,0:T(8,128)S(1)} %copy-done.1, bf16[256,2048]{1,0:T(8,128)(2,1)} %copy-done.2, bf16[256,2048]{1,0:T(8,128)(2,1)} %copy-done.4, f32[2048]{0:T(1024)S(1)} %div.11, f32[256]{0:T(256)S(1)} %bitcast.17, bf16[512,2048]{1,0:T(8,128)(2,1)} %copy-done.3), kind=kLoop, calls=%fused_computation.16 | loop fusion | flops 4718592 | bytes 9446400 | tf_op jit(solution)/shard_map/sub | solution.py:65
  (2 shorter events, 0.0 us)
Async XLA Ops:
  7.2 37.3 %copy-start = (bf16[512,512]{1,0:T(8,128)(2,1)S(1)}, bf16[512,512]{1,0:T(8,128)(2,1)}, u32[]{:S(2)}) copy-start(bf16[512,512]{1,0:T(8,128)(2,1)} %param.9) | copy-start | bytes 1572868
  7.2 3.2 %copy-start.1 = (f32[256,2048]{1,0:T(8,128)S(1)}, f32[256,2048]{1,0:T(8,128)}, u32[]{:S(2)}) copy-start(f32[256,2048]{1,0:T(8,128)} %param.7) | copy-start | bytes 6291460
  7.2 85.8 %all-gather.3.cloned.1.call-start = ((), (), s32[]{:S(2)}) async-start(), calls=%async_computation | async-start | bytes 2162688 | tf_op jit(solution)/shard_map/all_gather | solution.py:38
  10.6 1.0 copy-start.6
  11.5 32.9 %collective-permute-start = (bf16[256,2048]{1,0:T(8,128)(2,1)S(1)}, bf16[256,2048]{1,0:T(8,128)(2,1)}, u32[]{:S(2)}, u32[]{:S(2)}) collective-permute-start(bf16[256,2048]{1,0:T(8,128)(2,1)S(1)} %convert_element_type.39), channel_id=1, source_target_pairs={{0,1},{1,2},{2,3},{3,4},{4,5},{5,6},{6,7},{7,8},{8,9},{9,10},{10,1... | collective-permute-start | bytes 3145736 | tf_op jit(solution)/shard_map/ppermute | solution.py:10
  52.0 60.4 %copy-start.7 = (s32[1,8]{1,0:T(1,128)S(1)}, s32[1,8]{1,0:T(1,128)}, u32[]{:S(2)}) copy-start(s32[1,8]{1,0:T(1,128)} %param.11) | copy-start | bytes 100
  52.0 61.5 %collective-permute-start.1 = (bf16[256,2048]{1,0:T(8,128)(2,1)}, bf16[256,2048]{1,0:T(8,128)(2,1)}, u32[]{:S(2)}, u32[]{:S(2)}) collective-permute-start(bf16[256,2048]{1,0:T(8,128)(2,1)} %slice.17), channel_id=1, source_target_pairs={{0,31},{1,0},{2,1},{3,2},{4,3},{5,4},{6,5},{7,6},{8,7},{9,8},{10,9... | collective-permute-start | bytes 3145736 | tf_op jit(solution)/shard_map/ppermute | solution.py:10
  95.7 17.8 %copy-start.5 = (bf16[512,2048]{1,0:T(8,128)(2,1)S(1)}, bf16[512,2048]{1,0:T(8,128)(2,1)}, u32[]{:S(2)}) copy-start(bf16[512,2048]{1,0:T(8,128)(2,1)} %fusion) | copy-start | bytes 6291460
  113.5 31.2 %copy-start.8 = (bf16[512,512]{1,0:T(8,128)(2,1)S(1)}, bf16[512,512]{1,0:T(8,128)(2,1)}, u32[]{:S(2)}) copy-start(bf16[512,512]{1,0:T(8,128)(2,1)} %param.8) | copy-start | bytes 1572868
  115.4 54.7 %copy-start.2 = (bf16[256,2048]{1,0:T(8,128)(2,1)}, bf16[256,2048]{1,0:T(8,128)(2,1)S(1)}, u32[]{:S(2)}) copy-start(bf16[256,2048]{1,0:T(8,128)(2,1)S(1)} %get-tuple-element.5) | copy-start | bytes 3145732
  115.4 29.3 %collective-permute-start.2 = (bf16[256,2048]{1,0:T(8,128)(2,1)S(1)}, bf16[256,2048]{1,0:T(8,128)(2,1)S(1)}, u32[]{:S(2)}, u32[]{:S(2)}) collective-permute-start(bf16[256,2048]{1,0:T(8,128)(2,1)S(1)} %get-tuple-element.5), channel_id=1, source_target_pairs={{0,1},{1,2},{2,3},{3,4},{4,5},{5,6},{6,7},{7,8},{8,9},{9,10},{10,1... | collective-permute-start | bytes 3145736 | tf_op jit(solution)/shard_map/ppermute | solution.py:10
  146.0 24.9 %copy-start.3 = (bf16[512,2048]{1,0:T(8,128)(2,1)}, bf16[512,2048]{1,0:T(8,128)(2,1)S(1)}, u32[]{:S(2)}) copy-start(bf16[512,2048]{1,0:T(8,128)(2,1)S(1)} %fusion.1) | copy-start | bytes 6291460
  146.0 1.4 copy-start.9
  146.0 1.4 copy-start.10
  146.1 24.1 %collective-permute-start.3 = (bf16[256,2048]{1,0:T(8,128)(2,1)S(1)}, bf16[256,2048]{1,0:T(8,128)(2,1)S(1)}, u32[]{:S(2)}, u32[]{:S(2)}) collective-permute-start(bf16[256,2048]{1,0:T(8,128)(2,1)S(1)} %slice.19), channel_id=1, source_target_pairs={{0,31},{1,0},{2,1},{3,2},{4,3},{5,4},{6,5},{7,6},{8,7},{9,8},{10,9... | collective-permute-start | bytes 3145736 | tf_op jit(solution)/shard_map/ppermute | solution.py:10
  170.2 1.0 copy-start.4
Sparse Core Ops, SparseCore 0:
  10.6 82.3 all-gather.2
